TPU v7x, 32 devices: a whole 2x2x4 slice. The times are simulated.
32 devices in a mesh: crops: 1, rows: 16 (over z, y, core), cols: 2 (over x).
Axes of the slice: x: 2, y: 2, z: 4, core: 2. Of those that a mesh axis runs over, the one named last changes fastest.
Arguments:
- family_representation: float32 [128, 256, 256], P(('crops', 'rows'), 'cols'), may hold values from -6 to 6
- family_keep_flags: int32 [128, 256], P(('crops', 'rows'), 'cols'), may hold values 0 or 1
- amino_presence: int32 [256], P('crops'), may hold values 0 or 1
- contact_embedding: float32 [256, 256, 128], P(('crops', 'rows'), 'cols'), may hold values from -6 to 6
- couple_lhs_weights: bfloat16 [256, 32], replicated, may hold values from -0.375 to 0.375
- couple_rhs_weights: bfloat16 [256, 32], replicated, may hold values from -0.375 to 0.375
- pairwise_final_matrix: bfloat16 [1024, 128], replicated, may hold values from -1.5 to 1.5
- edge_source_matrix: bfloat16 [128, 256], replicated, may hold values from -0.5 to 0.5
- edge_target_matrix: bfloat16 [128, 256], replicated, may hold values from -0.5 to 0.5
- edge_final_sigmoid_matrix: bfloat16 [128, 128], replicated, may hold values from -0.5 to 0.5
- edge_final_matrix: bfloat16 [128, 128], replicated, may hold values from -0.5 to 0.5
- feedforward_expand_matrix: bfloat16 [128, 512], replicated, may hold values from -0.5 to 0.5
- feedforward_shrink_matrix: bfloat16 [512, 128], replicated, may hold values from -0.25 to 0.25
Outputs:
- pair_out: float32 [256, 256, 128], P(('crops', 'rows'), 'cols')
All inputs are finite; a program needn't handle non-finite values. No bound on the sum of `family_keep_flags` on one device may be relied on, other than what follows from the above.
Results may differ from a plain program's by a relative error of at most 0.0053.
Values may be sent and summed in bfloat16 or wider, within the bound.
A program may use at most 64 MiB of HBM per device.

v0:
```python
import jax
import jax.numpy as jnp
from jax import lax
from jax.sharding import PartitionSpec as P

epsilon = 1e-05


def normalise_features_step(values, reduce_axis):
    mean = jnp.mean(values, axis=reduce_axis, keepdims=True)
    centred = values - mean
    spread = jnp.mean(centred * centred, axis=reduce_axis, keepdims=True)
    return centred * lax.rsqrt(spread + epsilon)


def make_panel(normed_pair, weight, pair_live):
    raw = jnp.einsum("ijz,zc->cij", normed_pair, weight, preferred_element_type=jnp.float32)
    channels = raw.shape[0] // 2
    return (raw[:channels] * jax.nn.sigmoid(raw[channels:]) * pair_live[None]).astype(jnp.bfloat16)


def on_device(
    family_representation,
    family_keep_flags,
    amino_presence,
    contact_embedding,
    couple_lhs_weights,
    couple_rhs_weights,
    pairwise_final_matrix,
    edge_source_matrix,
    edge_target_matrix,
    edge_final_sigmoid_matrix,
    edge_final_matrix,
    feedforward_expand_matrix,
    feedforward_shrink_matrix,
):
    tile_rows = contact_embedding.shape[0]
    tile_cols = contact_embedding.shape[1]
    rows_count = lax.axis_size("rows")
    cols_count = lax.axis_size("cols")
    row_start = lax.axis_index("rows") * tile_rows
    col_start = lax.axis_index("cols") * tile_cols
    residue_float_mask = amino_presence.astype(jnp.float32)
    rows_live = lax.dynamic_slice_in_dim(residue_float_mask, row_start, tile_rows, 0)
    active_columns = lax.dynamic_slice_in_dim(residue_float_mask, col_start, tile_cols, 0)
    retained_family_entries = family_keep_flags.astype(jnp.float32) * active_columns[None, :]
    rescaled_family_rep = normalise_features_step(family_representation, -1).astype(jnp.bfloat16)
    family_lhs_mapped = (
        jnp.einsum(
            "ohp,pd->ohd",
            rescaled_family_rep,
            couple_lhs_weights,
            preferred_element_type=jnp.float32,
        )
        * retained_family_entries[:, :, None]
    ).astype(jnp.bfloat16)
    family_rhs_mapped = (
        jnp.einsum(
            "ohp,pd->ohd",
            rescaled_family_rep,
            couple_rhs_weights,
            preferred_element_type=jnp.float32,
        )
        * retained_family_entries[:, :, None]
    ).astype(jnp.bfloat16)
    live_half = retained_family_entries.astype(jnp.bfloat16)
    right_all, right_live = (
        lax.all_gather(family_rhs_mapped, "rows", axis=0, tiled=True),
        lax.all_gather(live_half, "rows", axis=0, tiled=True),
    )
    left_wide, wide_live = (
        lax.all_gather(family_lhs_mapped, "cols", axis=1, tiled=True),
        lax.all_gather(live_half, "cols", axis=1, tiled=True),
    )
    left_all, left_live = (
        lax.all_to_all(left_wide, "rows", split_axis=1, concat_axis=0, tiled=True),
        lax.all_to_all(wide_live, "rows", split_axis=1, concat_axis=0, tiled=True),
    )
    family_tally = left_all.shape[0]
    intermediate_breadth = left_all.shape[2]
    portion_number = min(8, tile_rows)
    count_blocks = tile_rows // portion_number
    port_portion_group = left_all.reshape(
        family_tally, count_blocks, portion_number, intermediate_breadth
    ).transpose(1, 0, 2, 3)
    live_blocks = left_live.reshape(family_tally, count_blocks, portion_number).transpose(1, 0, 2)

    def outer_block(item):
        port_segments, lives = item
        averaged_tensor_contraction = jnp.einsum(
            "lyj,lnx->ynjx", port_segments, right_all, preferred_element_type=jnp.float32
        )
        counts = jnp.einsum("si,sj->ij", lives, right_live, preferred_element_type=jnp.float32)
        mean = (averaged_tensor_contraction / jnp.maximum(counts, 1.0)[:, :, None, None]).astype(
            jnp.bfloat16
        )
        flat = mean.reshape(portion_number * tile_cols, intermediate_breadth * intermediate_breadth)
        return jnp.dot(flat, pairwise_final_matrix, preferred_element_type=jnp.float32).reshape(
            portion_number, tile_cols, -1
        )

    update = lax.map(outer_block, (port_portion_group, live_blocks))
    first = contact_embedding + update.reshape(tile_rows, tile_cols, -1)
    pair_normed = normalise_features_step(first, -1).astype(jnp.bfloat16)
    pair_live = rows_live[:, None] * active_columns[None, :]
    left_panel = make_panel(pair_normed, edge_source_matrix, pair_live)
    right_panel = make_panel(pair_normed, edge_target_matrix, pair_live)
    gate = jax.nn.sigmoid(
        jnp.dot(pair_normed, edge_final_sigmoid_matrix, preferred_element_type=jnp.float32)
    )
    left_recv, right_recv = (
        lax.all_to_all(left_panel, ("rows", "cols"), split_axis=0, concat_axis=1, tiled=True),
        lax.all_to_all(right_panel, ("rows", "cols"), split_axis=0, concat_axis=1, tiled=True),
    )
    owned = left_recv.shape[0]
    left_full = (
        left_recv.reshape(owned, rows_count, cols_count, tile_rows, tile_cols)
        .transpose(0, 1, 3, 2, 4)
        .reshape(owned, rows_count * tile_rows, cols_count * tile_cols)
    )
    right_full = (
        right_recv.reshape(owned, rows_count, cols_count, tile_rows, tile_cols)
        .transpose(0, 1, 3, 2, 4)
        .reshape(owned, rows_count * tile_rows, cols_count * tile_cols)
    )
    product = jnp.einsum(
        "cik,cjk->cij", left_full, right_full, preferred_element_type=jnp.float32
    ).astype(jnp.bfloat16)
    owned = product.shape[0]
    regrouped = (
        product.reshape(owned, rows_count, tile_rows, cols_count, tile_cols)
        .transpose(0, 1, 3, 2, 4)
        .reshape(owned, rows_count * cols_count * tile_rows, tile_cols)
    )
    returned = lax.all_to_all(regrouped, ("rows", "cols"), split_axis=1, concat_axis=0, tiled=True)
    mixed = normalise_features_step(returned.astype(jnp.float32), 0).astype(jnp.bfloat16)
    projected = jnp.einsum(
        "cij,cz->ijz", mixed, edge_final_matrix, preferred_element_type=jnp.float32
    )
    second = first + gate * projected
    trans_normed = normalise_features_step(second, -1).astype(jnp.bfloat16)
    hidden = jax.nn.relu(
        jnp.dot(trans_normed, feedforward_expand_matrix, preferred_element_type=jnp.float32)
    ).astype(jnp.bfloat16)
    return second + jnp.dot(hidden, feedforward_shrink_matrix, preferred_element_type=jnp.float32)


def solution(mesh):
    in_specs = (
        P(("crops", "rows"), "cols", None),
        P(("crops", "rows"), "cols"),
        P("crops"),
        P(("crops", "rows"), "cols", None),
        P(),
        P(),
        P(),
        P(),
        P(),
        P(),
        P(),
        P(),
        P(),
    )
    out_specs = P(("crops", "rows"), "cols", None)
    return jax.shard_map(
        on_device, mesh=mesh, in_specs=in_specs, out_specs=out_specs, check_vma=False
    )
```

profile of v0, /device:TPU:0, one launch (start us, length us, event | category | flops | bytes accessed | tf_op | source)
XLA Modules:
  0.0 145.3 jit_solution(2600993245930080658)
XLA Ops:
  6.6 0.8 convert_element_type.65
  7.4 1.4 reduce_sum.72
  8.8 1.6 %multiply_reduce_fusion.3 = f32[8,128]{1,0:T(8,128)S(1)} fusion(f32[8,128,256]{2,1,0:T(8,128)} %param.15, f32[8,128]{1,0:T(8,128)S(1)} %broadcast_multiply_fusion.4), kind=kLoop, calls=%fused_computation.52 | loop fusion | flops 785408 | bytes 1056768 | tf_op jit(solution)/shard_map/reduce_sum | solution.py:12
  10.5 1.1 fusion.18
  11.6 5.3 %all_gather.14 = bf16[8,256]{1,0:T(8,128)(2,1)S(1)} all-gather(bf16[8,128]{1,0:T(8,128)(2,1)S(1)} %get-tuple-element.94), channel_id=1, replica_groups=mesh['crops'=1,'rows'=16,'cols'=2] {'cols'}, dimensions={1}, use_global_device_ids=true | all-gather | bytes 6144 | tf_op jit(solution)/shard_map/all_gather | solution.py:73
  17.0 0.6 copy.105
  17.7 6.5 %all-to-all-start.1 = ((bf16[8,16,16]{2,0,1:T(8,128)(2,1)}), bf16[8,16,16]{2,0,1:T(8,128)(2,1)S(1)}, u32[]{:S(2)}, u32[]{:S(2)}) async-start(bf16[8,16,16]{2,0,1:T(8,128)(2,1)} %copy.105), calls=%async_computation.1 | async-start | bytes 65536 | tf_op jit(solution)/shard_map/all_to_all | solution.py:77
  24.6 5.1 %all_gather.12 = bf16[8,256,32]{1,2,0:T(8,128)(2,1)S(1)} all-gather(bf16[8,128,32]{1,2,0:T(8,128)(2,1)S(1)} %fusion.17), channel_id=1, replica_groups=mesh['crops'=1,'rows'=16,'cols'=2] {'cols'}, dimensions={1}, use_global_device_ids=true | all-gather | bytes 196608 | tf_op jit(solution)/shard_map/all_gather | solution.py:72
  30.1 1.2 reshape.150
  31.3 5.8 %all-to-all-start = ((bf16[16,2,2048]{2,1,0:T(2,128)(2,1)}), bf16[16,2,2048]{2,1,0:T(2,128)(2,1)S(1)}, u32[]{:S(2)}, u32[]{:S(2)}) async-start(bf16[16,2,2048]{2,1,0:T(2,128)(2,1)} %reshape.150), calls=%async_computation | async-start | bytes 262144 | tf_op jit(solution)/shard_map/all_to_all | solution.py:76
  37.6 21.8 %all_gather.15 = bf16[128,128]{1,0:T(8,128)(2,1)S(1)} all-gather(bf16[8,128]{1,0:T(8,128)(2,1)S(1)} %get-tuple-element.94), channel_id=1, replica_groups=mesh['crops'=1,'rows'=16,'cols'=2] {'rows'}, dimensions={0}, use_global_device_ids=true | all-gather | bytes 34816 | tf_op jit(solution)/shard_map/all_gather | solution.py:69
  60.5 2.6 %copy.108 = bf16[128,128,32]{1,0,2:T(8,128)(2,1)} copy(bf16[128,128,32]{1,2,0:T(8,128)(2,1)} %all-gather.2.cloned.1.call-done) | data formatting | bytes 2097152 | tf_op jit(solution)/shard_map/while | solution.py:102
  63.1 9.5 %while.10 = (s32[]{:T(128)}, f32[2,8,128,128]{2,3,1,0:T(8,128)}, bf16[2,128,8,32]{1,3,2,0:T(8,128)(2,1)S(1)}, bf16[128,128,32]{1,0,2:T(8,128)(2,1)}, bf16[2,128,...) while((s32[]{:T(128)}, f32[2,8,128,128]{2,3,1,0:T(8,128)}, ...), condition=%wide.region_3.4_spmd, body=%wide.region_2.3_spmd.sunk | while | flops 539231232 | bytes 18720920 | solution.py:102
  63.2 1.9 %fusion.72 = bf16[8,128,32,32]{1,2,3,0:T(8,128)(2,1)S(1)} fusion(f32[8,128]{1,0:T(8,128)S(1)} %convolution_maximum_fusion.2, bf16[128,128,32]{1,0,2:T(8,128)(2,1)} %get-tuple-element.165, bf16[2,128,8,32]{1,3,2,0:T(8,128)(2,1)S(1)} %get-tuple-element.164, s32[]{:T(128)} %get-tuple-element.154), kind=kOutput, calls=%fused_computation.1.clone.1 | convolution fusion | flops 270532608 | bytes 3215364 | tf_op jit(solution)/shard_map/while/body/eval_jaxpr/lyj,lnx->ynjx/dot_general | solution.py:90
  65.2 0.8 copy.160
  66.9 1.0 copy-done.4
  68.0 1.9 %fusion.72 = bf16[8,128,32,32]{1,2,3,0:T(8,128)(2,1)S(1)} fusion(f32[8,128]{1,0:T(8,128)S(1)} %convolution_maximum_fusion.2, bf16[128,128,32]{1,0,2:T(8,128)(2,1)} %get-tuple-element.165, bf16[2,128,8,32]{1,3,2,0:T(8,128)(2,1)S(1)} %get-tuple-element.164, s32[]{:T(128)} %get-tuple-element.154), kind=kOutput, calls=%fused_computation.1.clone.1 | convolution fusion | flops 270532608 | bytes 3215364 | tf_op jit(solution)/shard_map/while/body/eval_jaxpr/lyj,lnx->ynjx/dot_general | solution.py:90
  69.9 0.8 copy.160
  71.6 1.0 copy-done.4
  72.6 1.4 fusion.50
  75.3 0.6 fusion.32
  75.9 1.2 copy.114
  77.1 2.6 %all-to-all-start.2 = ((bf16[128,16,128]{2,1,0:T(8,128)(2,1)}), bf16[128,16,128]{2,1,0:T(8,128)(2,1)S(1)}, u32[]{:S(2)}, u32[]{:S(2)}) async-start(bf16[128,16,128]{2,1,0:T(8,128)(2,1)} %copy.114), calls=%async_computation.2 | async-start | bytes 1048576 | tf_op jit(solution)/shard_map/all_to_all | solution.py:112
  79.7 1.2 copy.117
  80.9 13.8 %all-to-all-done.2 = bf16[128,16,128]{2,1,0:T(8,128)(2,1)S(1)} async-done(((bf16[128,16,128]{2,1,0:T(8,128)(2,1)}), bf16[128,16,128]{2,1,0:T(8,128)(2,1)S(1)}, u32[]{:S(2)}, u32[]{:S(2)}) %all-to-all-start.2) | async-done | bytes 524320 | tf_op jit(solution)/shard_map/all_to_all | solution.py:112
  94.7 3.7 %all-to-all-start.3 = ((bf16[128,16,128]{2,1,0:T(8,128)(2,1)}), bf16[128,16,128]{2,1,0:T(8,128)(2,1)S(1)}, u32[]{:S(2)}, u32[]{:S(2)}) async-start(bf16[128,16,128]{2,1,0:T(8,128)(2,1)} %copy.117), calls=%async_computation.3 | async-start | bytes 1048576 | tf_op jit(solution)/shard_map/all_to_all | solution.py:113
  98.4 0.5 copy.158
  99.3 13.9 %all-to-all-done.3 = bf16[128,16,128]{2,1,0:T(8,128)(2,1)S(1)} async-done(((bf16[128,16,128]{2,1,0:T(8,128)(2,1)}), bf16[128,16,128]{2,1,0:T(8,128)(2,1)S(1)}, u32[]{:S(2)}, u32[]{:S(2)}) %all-to-all-start.3) | async-done | bytes 524320 | tf_op jit(solution)/shard_map/all_to_all | solution.py:113
  113.2 0.5 copy.157
  115.1 18.4 %all_to_all.70 = bf16[4,512,128]{2,0,1:T(4,128)(2,1)S(1)} all-to-all(bf16[4,512,128]{2,0,1:T(4,128)(2,1)S(1)} %copy.120), channel_id=1, replica_groups=mesh['crops'=1,'rows'=16,'cols'=2] {'rows','cols'}, dimensions={1} | all-to-all | bytes 1048576 | tf_op jit(solution)/shard_map/all_to_all | solution.py:135
  135.8 1.3 fusion.12
  137.2 1.3 copy.127
  (77 shorter events, 9.7 us)
Async XLA Ops:
  6.5 129.1 %copy-start = (bf16[512,128]{1,0:T(8,128)(2,1)S(1)}, bf16[512,128]{1,0:T(8,128)(2,1)}, u32[]{:S(2)}) copy-start(bf16[512,128]{1,0:T(8,128)(2,1)} %param.27) | copy-start | bytes 393220
  6.5 4.0 %copy-start.1 = (f32[8,128,256]{2,1,0:T(8,128)S(1)}, f32[8,128,256]{2,1,0:T(8,128)}, u32[]{:S(2)}) copy-start(f32[8,128,256]{2,1,0:T(8,128)} %param.15) | copy-start | bytes 3145732
  6.5 4.0 %copy-start.12 = (s32[8,128]{1,0:T(8,128)S(1)}, s32[8,128]{1,0:T(8,128)}, u32[]{:S(2)}) copy-start(s32[8,128]{1,0:T(8,128)} %param.16) | copy-start | bytes 12292
  6.5 4.0 %copy-start.10 = (bf16[256,32]{0,1:T(8,128)(2,1)S(1)}, bf16[256,32]{0,1:T(8,128)(2,1)}, u32[]{:S(2)}) copy-start(bf16[256,32]{0,1:T(8,128)(2,1)} %param.20) | copy-start | bytes 49156
  6.5 17.6 %copy-start.11 = (bf16[256,32]{0,1:T(8,128)(2,1)S(1)}, bf16[256,32]{0,1:T(8,128)(2,1)}, u32[]{:S(2)}) copy-start(bf16[256,32]{0,1:T(8,128)(2,1)} %param.19) | copy-start | bytes 49156
  6.5 53.9 %all-gather.2.cloned.1.call-start = ((), (), s32[]{:S(2)}) async-start(), calls=%async_computation.5 | async-start | bytes 1114112 | tf_op jit(solution)/shard_map/all_gather | solution.py:68
  10.5 26.6 %copy-start.5 = (f32[16,128,128]{2,1,0:T(8,128)S(1)}, f32[16,128,128]{2,1,0:T(8,128)}, u32[]{:S(2)}) copy-start(f32[16,128,128]{2,1,0:T(8,128)} %param.18) | copy-start | bytes 3145732
  17.7 13.6 %all-to-all-start.1 = ((bf16[8,16,16]{2,0,1:T(8,128)(2,1)}), bf16[8,16,16]{2,0,1:T(8,128)(2,1)S(1)}, u32[]{:S(2)}, u32[]{:S(2)}) async-start(bf16[8,16,16]{2,0,1:T(8,128)(2,1)} %copy.105), calls=%async_computation.1 | async-start | bytes 65536 | tf_op jit(solution)/shard_map/all_to_all | solution.py:77
  31.3 28.3 %all-to-all-start = ((bf16[16,2,2048]{2,1,0:T(2,128)(2,1)}), bf16[16,2,2048]{2,1,0:T(2,128)(2,1)S(1)}, u32[]{:S(2)}, u32[]{:S(2)}) async-start(bf16[16,2,2048]{2,1,0:T(2,128)(2,1)} %reshape.150), calls=%async_computation | async-start | bytes 262144 | tf_op jit(solution)/shard_map/all_to_all | solution.py:76
  59.6 3.5 %copy-start.2 = (bf16[1024,128]{1,0:T(8,128)(2,1)S(1)}, bf16[1024,128]{1,0:T(8,128)(2,1)}, u32[]{:S(2)}) copy-start(bf16[1024,128]{1,0:T(8,128)(2,1)} %param.21) | copy-start | bytes 786436
  65.1 1.2 copy-start.3
  66.9 1.0 copy-start.4
  69.9 1.2 copy-start.3
  71.6 1.0 copy-start.4
  72.6 1.6 %copy-start.7 = (bf16[128,256]{1,0:T(8,128)(2,1)S(1)}, bf16[128,256]{1,0:T(8,128)(2,1)}, u32[]{:S(2)}) copy-start(bf16[128,256]{1,0:T(8,128)(2,1)} %param.22) | copy-start | bytes 196612
  74.0 0.8 copy-start.8
  77.1 17.6 %all-to-all-start.2 = ((bf16[128,16,128]{2,1,0:T(8,128)(2,1)}), bf16[128,16,128]{2,1,0:T(8,128)(2,1)S(1)}, u32[]{:S(2)}, u32[]{:S(2)}) async-start(bf16[128,16,128]{2,1,0:T(8,128)(2,1)} %copy.114), calls=%async_computation.2 | async-start | bytes 1048576 | tf_op jit(solution)/shard_map/all_to_all | solution.py:112
  94.7 18.5 %all-to-all-start.3 = ((bf16[128,16,128]{2,1,0:T(8,128)(2,1)}), bf16[128,16,128]{2,1,0:T(8,128)(2,1)S(1)}, u32[]{:S(2)}, u32[]{:S(2)}) async-start(bf16[128,16,128]{2,1,0:T(8,128)(2,1)} %copy.117), calls=%async_computation.3 | async-start | bytes 1048576 | tf_op jit(solution)/shard_map/all_to_all | solution.py:113
  133.8 0.8 copy-start.9
  134.1 0.8 copy-start.13
  134.9 0.9 copy-start.6
Sparse Core Ops, SparseCore 0:
  11.8 41.4 all-gather.1
where the time goes:
time: 147 us; the launch traced here: 145 us
  blocking collectives  50.6 us (34%)
  waiting for transfers between devices  27.7 us (19%)
  starting transfers between devices  18.7 us (13%)
  local copies, waits for them, and re-layouts  17.6 us (12%)
  between operations  13.8 us (9%)
  matrix products  10.1 us (7%)
  other arithmetic  6.74 us (5%)
    all_gather x1, blocking collectives, on_device(): lax.all_gather(live_half, 'rows', axis=0, tiled=True)  21.8 us
    all_to_all x1, blocking collectives, on_device(): lax.all_to_all(regrouped, ('rows', 'cols'), split_axis=1, concat_axis=0,...  18.4 us
    all_to_all x1, waiting for transfers between devices, on_device(): lax.all_to_all(right_panel, ('rows', 'cols'), split_axis=0, concat_axis=1...  13.9 us
    all_to_all x1, waiting for transfers between devices, on_device(): lax.all_to_all(left_panel, ('rows', 'cols'), split_axis=0, concat_axis=1,...  13.8 us
    all_to_all x1, starting transfers between devices, on_device(): lax.all_to_all(wide_live, 'rows', split_axis=1, concat_axis=0, tiled=True)  6.49 us
    all_to_all x1, starting transfers between devices, on_device(): lax.all_to_all(left_wide, 'rows', split_axis=1, concat_axis=0, tiled=True)  5.84 us
    all_gather x1, blocking collectives, on_device(): lax.all_gather(live_half, 'cols', axis=1, tiled=True)  5.29 us
    all_gather x1, blocking collectives, on_device(): lax.all_gather(family_lhs_mapped, 'cols', axis=1, tiled=True)  5.13 us
  transfers between devices with their start and end apart: 5, of which 2 were waited for; matrix products, arithmetic and copies ran while one was open for 4% of the time, Pallas kernels for 0%

commit v1 on v0

v1 whole, which is shorter than its diff:
```python
import functools

import jax
import jax.numpy as jnp
from jax import lax
from jax.experimental import pallas as pl
from jax.experimental.pallas import tpu as pltpu
from jax.sharding import PartitionSpec as P

EPS = 1e-05
F32 = jnp.float32
BF16 = jnp.bfloat16
MESH = pl.DeviceIdType.MESH
VM = pl.BlockSpec(memory_space=pltpu.VMEM)
SM = pl.BlockSpec(memory_space=pltpu.SMEM)
ANY = pl.BlockSpec(memory_space=pl.ANY)
PACK = 4


def contract(a, b, da, db):
    return lax.dot_general(a, b, (((da,), (db,)), ((), ())), preferred_element_type=F32)


def normalise(v, axis):
    mean = jnp.mean(v, axis=axis, keepdims=True)
    cen = v - mean
    var = jnp.mean(cen * cen, axis=axis, keepdims=True)
    return cen * lax.rsqrt(var + EPS)


def project_kernel(fam, keep, amino, wl, wr, rsend, lsend, rsc):
    ns, tc, _ = fam.shape
    ch = wl.shape[1]
    x = lax.axis_index("cols")
    cols_live = amino[:, pl.ds(pl.multiple_of(x * tc, tc), tc)].astype(F32)
    live = keep[...].astype(F32) * cols_live
    live_t = live.T
    for g in range(ns // PACK):
        parts = []
        for k in range(PACK):
            s = g * PACK + k
            xn = normalise(fam[s], -1).astype(BF16)
            rt = contract(wr[...], xn, 0, 1) * live[s : s + 1, :]
            rsc[pl.ds(s, ch, stride=ns), :] = rt
            parts.append(
                jnp.dot(xn, wl[...], preferred_element_type=F32) * live_t[:, s : s + 1]
            )
        lsend[g] = jnp.concatenate(parts, axis=1).astype(BF16)
    rsend[0:ch] = rsc[...].reshape(ch, ns, tc).astype(BF16)
    rsend[ch] = live.astype(BF16)


def full_barrier(rows, cols, r, x):
    n = rows * cols
    me = r * cols + x
    barrier = pltpu.get_barrier_semaphore()

    def greet(t, carry):
        other = lax.rem(me + t, n)
        pl.semaphore_signal(
            barrier,
            inc=1,
            device_id={"rows": other // cols, "cols": lax.rem(other, cols)},
            device_id_type=MESH,
        )
        return carry

    lax.fori_loop(1, n, greet, 0)
    pl.semaphore_wait(barrier, n - 1)


def opm_exchange_kernel(
    rows, cols, tr, rsend, lsend, rbuf, lbuf, vbuf,
    rs_send, rs_recv, ls_send, ls_recv, vs_send, vs_recv, local
):
    r = lax.axis_index("rows")
    x = lax.axis_index("cols")
    ch = rsend.shape[0] - 1
    tc = lsend.shape[1]
    rpc = tc // tr
    outer = rows // 4
    o = r // 4
    m = lax.rem(r // 2, 2)
    k = lax.rem(r, 2)
    full_barrier(rows, cols, r, x)

    def row_of(oo, mm, kk):
        return (oo * 2 + mm) * 2 + kk

    def rcopy(block, dst_row, sem, first):
        return pltpu.make_async_remote_copy(
            src_ref=rsend if first else rbuf.at[block],
            dst_ref=rbuf.at[block],
            send_sem=rs_send.at[sem],
            recv_sem=rs_recv.at[block],
            device_id={"rows": dst_row},
            device_id_type=MESH,
        )

    def rwait(block):
        pltpu.make_async_copy(rsend, rbuf.at[block], rs_recv.at[block]).wait()

    mate = row_of(o, m, 1 - k)
    side = row_of(o, 1 - m, k)
    sends = []
    for t in range(1, outer):
        sends.append(rcopy(r, row_of(lax.rem(o + t, outer), m, k), t - 1, True))
        sends[-1].start()
    sends.append(rcopy(r, side, outer - 1, True))
    sends[-1].start()
    sends.append(rcopy(r, mate, outer, True))
    sends[-1].start()
    own_r = pltpu.make_async_copy(rsend, rbuf.at[r], local.at[0])
    own_r.start()

    def lcopy(t, xx):
        return pltpu.make_async_remote_copy(
            src_ref=lsend.at[:, pl.ds(pl.multiple_of(t * tr, tr), tr), :],
            dst_ref=lbuf.at[r],
            send_sem=ls_send.at[t * cols + xx],
            recv_sem=ls_recv.at[r],
            device_id={"rows": x * rpc + t, "cols": xx},
            device_id_type=MESH,
        )

    def vcopy(t, xx):
        return pltpu.make_async_remote_copy(
            src_ref=rsend.at[ch],
            dst_ref=vbuf.at[r],
            send_sem=vs_send.at[t * cols + xx],
            recv_sem=vs_recv.at[r],
            device_id={"rows": x * rpc + t, "cols": xx},
            device_id_type=MESH,
        )

    mine = lax.rem(r, rpc)
    home = r // rpc

    def lsends(q, carry):
        t = q // cols
        xx = lax.rem(q, cols)

        @pl.when(jnp.logical_not(jnp.logical_and(x * rpc + t == r, xx == x)))
        def _():
            vcopy(t, xx).start()
            lcopy(t, xx).start()

        return carry

    lax.fori_loop(0, rpc * cols, lsends, 0)

    @pl.when(home == x)
    def _():
        a = pltpu.make_async_copy(
            lsend.at[:, pl.ds(pl.multiple_of(mine * tr, tr), tr), :], lbuf.at[r], local.at[1]
        )
        b = pltpu.make_async_copy(rsend.at[ch], vbuf.at[r], local.at[2])
        a.start()
        b.start()
        a.wait()
        b.wait()

    sem = outer + 1
    for t in range(1, outer):
        block = row_of(lax.rem(o + outer - t, outer), m, k)
        rwait(block)
        for dst in (side, mate):
            sends.append(rcopy(block, dst, sem, False))
            sends[-1].start()
            sem += 1
    for t in range(outer):
        block = row_of(lax.rem(o + outer - t, outer), 1 - m, k)
        rwait(block)
        sends.append(rcopy(block, mate, sem, False))
        sends[-1].start()
        sem += 1
    for t in range(outer):
        for mm in range(2):
            rwait(row_of(lax.rem(o + outer - t, outer), mm, 1 - k))
    own_r.wait()
    for s in sends:
        s.wait_send()

    def lwaits(q, carry):
        t = q // cols
        xx = lax.rem(q, cols)

        @pl.when(jnp.logical_not(jnp.logical_and(x * rpc + t == r, xx == x)))
        def _():
            vcopy(t, xx).wait_send()
            lcopy(t, xx).wait_send()

        return carry

    lax.fori_loop(0, rpc * cols, lwaits, 0)

    def lrecvs(src, carry):
        @pl.when(jnp.logical_not(jnp.logical_and(src == r, home == x)))
        def _():
            pltpu.make_async_copy(
                lsend.at[:, pl.ds(0, tr), :], lbuf.at[src], ls_recv.at[src]
            ).wait()
            pltpu.make_async_copy(rsend.at[ch], vbuf.at[src], vs_recv.at[src]).wait()

        return carry

    lax.fori_loop(0, rows, lrecvs, 0)


def outer_kernel(
    amino, amino_v, rbuf, lbuf, vbuf, contact, w2t, es, et, efs,
    lp, rp, first, gate, lf, lmat, cnts, acts, lsc, rsc
):
    rows, groups, tr, lanes = lbuf.shape
    ns = rbuf.shape[2]
    ch = rbuf.shape[1] - 1
    tc = rbuf.shape[3]
    total = rows * ns
    rg = rows * groups
    rpc = tc // tr
    zc = es.shape[1] // 2
    r = lax.axis_index("rows")
    x = lax.axis_index("cols")
    lf[...] = lbuf[...].astype(F32).reshape(rg * tr, lanes)
    place = (
        lax.broadcasted_iota(jnp.int32, (rg, total), 1) // PACK
        == lax.broadcasted_iota(jnp.int32, (rg, total), 0)
    ).astype(F32).astype(BF16)
    keep = lax.rem(
        lax.broadcasted_iota(jnp.int32, (lanes, total), 1), PACK
    ) == lax.broadcasted_iota(jnp.int32, (lanes, total), 0) // ch
    for i in range(tr):
        t = lf[pl.ds(i, rg, stride=tr), :].astype(BF16)
        y = jnp.where(keep, contract(t, place, 0, 0), 0.0)
        acc = y[0:ch]
        for q in range(1, PACK):
            acc = acc + y[q * ch : (q + 1) * ch]
        lmat[i * ch : (i + 1) * ch, :] = acc.astype(BF16)
    v_left = vbuf[...].astype(F32).reshape(total, tc).astype(BF16)
    v_right = rbuf[:, ch].astype(F32).reshape(total, tc).astype(BF16)
    cnts[...] = contract(v_left, v_right, 0, 0)
    own = lax.rem(r, rpc)
    inv = 1.0 / jnp.maximum(cnts[pl.ds(pl.multiple_of(own * tr, tr), tr), :], 1.0)

    def outer(d, carry):
        rd = rbuf[:, d].astype(F32).reshape(total, tc).astype(BF16)
        a = jnp.dot(lmat[...], rd, preferred_element_type=F32).reshape(tr, ch, tc)
        acts[:, pl.ds(pl.multiple_of(d * ch, ch), ch), :] = (a * inv[:, None, :]).astype(BF16)
        return carry

    lax.fori_loop(0, ch, outer, 0, unroll=4)
    cols_live = amino_v[:, pl.ds(pl.multiple_of(x * tc, tc), tc)].astype(F32)

    for i in range(tr):
        f = contact[i].T + jnp.dot(w2t[...], acts[i], preferred_element_type=F32)
        first[i] = f
        pn = normalise(f, 0).astype(BF16)
        mask = cols_live * amino[r * tr + i].astype(F32)
        raw = contract(es[...], pn, 0, 0)
        lsc[pl.ds(i, zc, stride=tr), :] = raw[:zc] * jax.nn.sigmoid(raw[zc:]) * mask
        raw = contract(et[...], pn, 0, 0)
        rsc[pl.ds(i, zc, stride=tr), :] = raw[:zc] * jax.nn.sigmoid(raw[zc:]) * mask
        gate[i] = jax.nn.sigmoid(contract(efs[...], pn, 0, 0))
    lp[...] = lsc[...].reshape(zc, tr, tc).astype(BF16)
    rp[...] = rsc[...].reshape(zc, tr, tc).astype(BF16)


def triangle_kernel(
    rows, cols, lp, rp, pbuf, lfull, rfull, prod,
    l_send, l_recv, r_send, r_recv, p_send, p_recv, local
):
    r = lax.axis_index("rows")
    x = lax.axis_index("cols")
    n = rows * cols
    me = r * cols + x
    own = lfull.shape[0]
    tr, tc = lp.shape[1:]
    full_barrier(rows, cols, r, x)

    def tile(ref, rr, xx):
        return ref.at[
            :, pl.ds(pl.multiple_of(rr * tr, tr), tr), pl.ds(pl.multiple_of(xx * tc, tc), tc)
        ]

    def panel(src, dst, t, send, recv):
        other = lax.rem(me + t, n)
        return pltpu.make_async_remote_copy(
            src_ref=src.at[pl.ds(other * own, own)],
            dst_ref=tile(dst, r, x),
            send_sem=send.at[t],
            recv_sem=recv.at[t],
            device_id={"rows": other // cols, "cols": lax.rem(other, cols)},
            device_id_type=MESH,
        )

    def back(t):
        other = lax.rem(me + t, n)
        rr = other // cols
        xx = lax.rem(other, cols)
        return pltpu.make_async_remote_copy(
            src_ref=tile(prod, rr, xx),
            dst_ref=pbuf.at[pl.ds(me * own, own)],
            send_sem=p_send.at[t],
            recv_sem=p_recv.at[t],
            device_id={"rows": rr, "cols": xx},
            device_id_type=MESH,
        )

    def start(t, carry):
        panel(lp, lfull, t, l_send, l_recv).start()
        panel(rp, rfull, t, r_send, r_recv).start()
        return carry

    lax.fori_loop(1, n, start, 0)
    a = pltpu.make_async_copy(lp.at[pl.ds(me * own, own)], tile(lfull, r, x), local.at[0])
    b = pltpu.make_async_copy(rp.at[pl.ds(me * own, own)], tile(rfull, r, x), local.at[1])
    a.start()
    b.start()
    a.wait()
    b.wait()

    def finish(t, carry):
        src = lax.rem(me + n - t, n)
        rr = src // cols
        xx = lax.rem(src, cols)
        pltpu.make_async_copy(lp.at[pl.ds(0, own)], tile(lfull, rr, xx), l_recv.at[t]).wait()
        pltpu.make_async_copy(rp.at[pl.ds(0, own)], tile(rfull, rr, xx), r_recv.at[t]).wait()
        return carry

    lax.fori_loop(1, n, finish, 0)
    for c in range(own):
        prod[c] = contract(lfull[c], rfull[c], 1, 1).astype(BF16)

    def send_back(t, carry):
        back(t).start()
        return carry

    lax.fori_loop(1, n, send_back, 0)
    a = pltpu.make_async_copy(tile(prod, r, x), pbuf.at[pl.ds(me * own, own)], local.at[0])
    a.start()
    a.wait()

    def drain(t, carry):
        src = lax.rem(me + n - t, n)
        pltpu.make_async_copy(
            lp.at[pl.ds(0, own)], pbuf.at[pl.ds(src * own, own)], p_recv.at[t]
        ).wait()
        panel(lp, lfull, t, l_send, l_recv).wait_send()
        panel(rp, rfull, t, r_send, r_recv).wait_send()
        back(t).wait_send()
        return carry

    lax.fori_loop(1, n, drain, 0)


def final_kernel(pbuf, first, gate, ef, fe, fs, out, sc):
    zc, tr, tc = pbuf.shape
    sc[...] = normalise(pbuf[...].astype(F32), 0).reshape(zc * tr, tc)
    for i in range(tr):
        mixed = sc[pl.ds(i, zc, stride=tr), :].astype(BF16)
        second = first[i] + gate[i] * contract(ef[...], mixed, 0, 0)
        tn = normalise(second, 0).astype(BF16)
        hidden = jax.nn.relu(contract(fe[...], tn, 0, 0)).astype(BF16)
        out[i] = (second + contract(fs[...], hidden, 0, 0)).T


def params(**kw):
    return pltpu.CompilerParams(vmem_limit_bytes=60 * 1024 * 1024, **kw)


def on_device(fam, keep, amino, contact, wl, wr, pf, es, et, efs, ef, fe, fs):
    rows = lax.axis_size("rows")
    cols = lax.axis_size("cols")
    ns, tc, _ = fam.shape
    tr = contact.shape[0]
    ch = wl.shape[1]
    z = contact.shape[2]
    zc = es.shape[1] // 2
    groups = ns // PACK
    lanes = PACK * ch
    n = rows * cols
    own = zc // n
    rpc = tc // tr
    total = rows * ns
    dma = pltpu.SemaphoreType.DMA
    amino_v = amino.reshape(1, -1)
    w2t = pf.reshape(ch, ch, z).transpose(2, 1, 0).reshape(z, ch * ch)
    sds = jax.ShapeDtypeStruct
    rsend, lsend = pl.pallas_call(
        project_kernel,
        out_shape=(sds((ch + 1, ns, tc), BF16), sds((groups, tc, lanes), BF16)),
        in_specs=[VM] * 5,
        out_specs=(VM, VM),
        scratch_shapes=[pltpu.VMEM((ch * ns, tc), F32)],
        compiler_params=params(),
        name="project",
    )(fam, keep, amino_v, wl, wr)
    nsem = (rows // 4) + 1 + 2 * (rows // 4 - 1) + rows // 4
    rbuf, lbuf, vbuf = pl.pallas_call(
        functools.partial(opm_exchange_kernel, rows, cols, tr),
        out_shape=(
            sds((rows, ch + 1, ns, tc), BF16),
            sds((rows, groups, tr, lanes), BF16),
            sds((rows, ns, tc), BF16),
        ),
        in_specs=[VM, VM],
        out_specs=(VM, VM, VM),
        scratch_shapes=[
            dma((nsem,)), dma((rows,)), dma((rpc * cols,)), dma((rows,)),
            dma((rpc * cols,)), dma((rows,)), dma((3,)),
        ],
        compiler_params=params(collective_id=0, has_side_effects=True),
        name="opm_exchange",
    )(rsend, lsend)
    lp, rp, first, gate = pl.pallas_call(
        outer_kernel,
        out_shape=(
            sds((zc, tr, tc), BF16), sds((zc, tr, tc), BF16),
            sds((tr, z, tc), F32), sds((tr, z, tc), F32),
        ),
        in_specs=[SM] + [VM] * 9,
        out_specs=(VM,) * 4,
        scratch_shapes=[
            pltpu.VMEM((rows * groups * tr, lanes), F32),
            pltpu.VMEM((tr * ch, total), BF16),
            pltpu.VMEM((tc, tc), F32),
            pltpu.VMEM((tr, ch * ch, tc), BF16),
            pltpu.VMEM((zc * tr, tc), F32),
            pltpu.VMEM((zc * tr, tc), F32),
        ],
        compiler_params=params(),
        name="outer",
    )(amino, amino_v, rbuf, lbuf, vbuf, contact, w2t, es, et, efs)
    pbuf = pl.pallas_call(
        functools.partial(triangle_kernel, rows, cols),
        out_shape=sds((zc, tr, tc), BF16),
        in_specs=[VM, VM],
        out_specs=VM,
        scratch_shapes=[
            pltpu.VMEM((own, rows * tr, cols * tc), BF16),
            pltpu.VMEM((own, rows * tr, cols * tc), BF16),
            pltpu.VMEM((own, rows * tr, cols * tc), BF16),
        ] + [dma((n,))] * 6 + [dma((2,))],
        compiler_params=params(collective_id=1, has_side_effects=True),
        name="triangle",
    )(lp, rp)
    return pl.pallas_call(
        final_kernel,
        out_shape=sds((tr, tc, z), F32),
        in_specs=[VM] * 6,
        out_specs=VM,
        scratch_shapes=[pltpu.VMEM((zc * tr, tc), F32)],
        compiler_params=params(),
        name="final",
    )(pbuf, first, gate, ef, fe, fs)


def solution(mesh):
    tile3 = P(("crops", "rows"), "cols", None)
    in_specs = (tile3, P(("crops", "rows"), "cols"), P("crops"), tile3) + (P(),) * 9
    return jax.shard_map(
        on_device, mesh=mesh, in_specs=in_specs, out_specs=tile3, check_vma=False
    )
```

time: 147 us -> 100 us (0.68)
  the two profiles are of different devices: /device:TPU:0 before, /device:TPU:21 now
where the time goes in v1:
time: 100 us; the launch traced here: 99.6 us
  Pallas kernels  95.8 us (96%)
  local copies, waits for them, and re-layouts  3.86 us (4%)
    pallas_call x1, Pallas kernels, on_device(): pl.pallas_call(functools.partial(triangle_kernel, rows, cols), out_shape=...  52.2 us
    pallas_call x1, Pallas kernels, on_device(): pl.pallas_call(functools.partial(opm_exchange_kernel, rows, cols, tr), ou...  20.1 us
    pallas_call x1, Pallas kernels, on_device(): pl.pallas_call(outer_kernel, out_shape=(sds((zc, tr, tc), BF16), sds((zc,...  12.1 us
    pallas_call x1, Pallas kernels, on_device(): pl.pallas_call(final_kernel, out_shape=sds((tr, tc, z), F32), in_specs=[V...  7.84 us
    pallas_call x1, Pallas kernels, on_device(): pl.pallas_call(project_kernel, out_shape=(sds((ch + 1, ns, tc), BF16), sd...  3.59 us
    unnamed x4, local copies, waits for them, and re-layouts  2.92 us

profile of v1, /device:TPU:21, one launch (start us, length us, event | category | flops | bytes accessed | tf_op | source)
XLA Modules:
  0.0 99.6 jit_solution(18138255305790006089)
XLA Ops:
  0.0 0.0 copy-start
  0.0 1.5 %copy.20.wl = bf16[256,32]{1,0:T(8,128)(2,1)} copy(bf16[256,32]{0,1:T(8,128)(2,1)} %param.17) | data formatting | bytes 32768 | tf_op args[4]
  1.5 1.4 %copy.21.wr = bf16[256,32]{1,0:T(8,128)(2,1)} copy(bf16[256,32]{0,1:T(8,128)(2,1)} %param.18) | data formatting | bytes 32768 | tf_op args[5]
  2.9 3.6 %project.1 = (bf16[33,8,128]{2,1,0:T(8,128)(2,1)}, bf16[2,128,128]{2,1,0:T(8,128)(2,1)}) custom-call(f32[8,128,256]{2,1,0:T(8,128)} %fam.1, s32[8,128]{1,0:T(8,128)} %keep.1, s32[1,256]{1,0:T(1,128)} %bitcast.7, bf16[256,32]{1,0:T(8,128)(2,1)} %copy.20.wl, bf16[256,32]{1,0:T(8,128)(2,1)} %copy.21.wr), custom_call_target="tpu_custom_call" | custom-call | tf_op jit(solution)/shard_map/project/pallas_call | solution.py:389
  6.5 0.0 copy-done
  6.5 0.1 copy.22
  6.6 0.8 copy.23.w2t
  7.5 20.1 %opm_exchange.1 = (bf16[16,33,8,128]{3,2,1,0:T(8,128)(2,1)}, bf16[16,2,16,128]{3,2,1,0:T(8,128)(2,1)}, bf16[16,8,128]{2,1,0:T(8,128)(2,1)}) custom-call(bf16[33,8,128]{2,1,0:T(8,128)(2,1)} %get-tuple-element.14.rsend, bf16[2,128,128]{2,1,0:T(8,128)(2,1)} %get-tuple-element.15.lsend), custom_call_target="tpu_custom_call" | custom-call | tf_op jit(solution)/shard_map/opm_exchange/pallas_call | solution.py:399
  27.6 12.1 %outer.1 = (bf16[128,16,128]{2,1,0:T(8,128)(2,1)}, bf16[128,16,128]{2,1,0:T(8,128)(2,1)}, f32[16,128,128]{2,1,0:T(8,128)}, f32[16,128,128]{2,1,0:T(8,128)}) custom-call(s32[256]{0:T(256)} %amino.1, s32[1,256]{1,0:T(1,128)} %bitcast.8, bf16[16,33,8,128]{3,2,1,0:T(8,128)(2,1)} %get-tuple-element.16.rbuf, bf16[16,2,16,128]{3,2,1,0:T(8,128)(2,1)} %get-tuple-element.17.lbuf, ...), custom_call_target="tpu_custom_call" | custom-call | tf_op jit(solution)/shard_map/outer/pallas_call | solution.py:415
  39.6 52.2 %triangle.1.pbuf = bf16[128,16,128]{2,1,0:T(8,128)(2,1)} custom-call(bf16[128,16,128]{2,1,0:T(8,128)(2,1)} %get-tuple-element.19.lp, bf16[128,16,128]{2,1,0:T(8,128)(2,1)} %get-tuple-element.20.rp), custom_call_target="tpu_custom_call" | custom-call | tf_op jit(solution)/shard_map/triangle/pallas_call | solution.py:434
  91.8 7.8 %final.1 = f32[16,128,128]{2,1,0:T(8,128)} custom-call(bf16[128,16,128]{2,1,0:T(8,128)(2,1)} %triangle.1.pbuf, f32[16,128,128]{2,1,0:T(8,128)} %get-tuple-element.21.first, f32[16,128,128]{2,1,0:T(8,128)} %get-tuple-element.22.gate, bf16[128,128]{1,0:T(8,128)(2,1)} %ef.1, bf16[128,512]{1,0:T(8,128)(2,1)} %fe.1, bf16[512,128]{1,0:T(8,128)(2,1)} %fs.1), custom_call_target="tpu_custom_call" | custom-call | tf_op jit(solution)/shard_map/final/pallas_call | solution.py:447
Async XLA Ops:
  0.0 6.5 %copy-start = (bf16[1024,128]{1,0:T(8,128)(2,1)S(1)}, bf16[1024,128]{1,0:T(8,128)(2,1)}, u32[]{:S(2)}) copy-start(bf16[1024,128]{1,0:T(8,128)(2,1)} %param.19) | copy-start | bytes 786436

commit v2 on v1

v2 whole, which is shorter than its diff:
```python
import functools

import jax
import jax.numpy as jnp
from jax import lax
from jax.experimental import pallas as pl
from jax.experimental.pallas import tpu as pltpu
from jax.sharding import PartitionSpec as P

EPS = 1e-05
F32 = jnp.float32
BF16 = jnp.bfloat16
MESH = pl.DeviceIdType.MESH
VM = pl.BlockSpec(memory_space=pltpu.VMEM)
SM = pl.BlockSpec(memory_space=pltpu.SMEM)
ANY = pl.BlockSpec(memory_space=pl.ANY)
PACK = 4


def contract(a, b, da, db):
    return lax.dot_general(a, b, (((da,), (db,)), ((), ())), preferred_element_type=F32)


def normalise(v, axis):
    mean = jnp.mean(v, axis=axis, keepdims=True)
    cen = v - mean
    var = jnp.mean(cen * cen, axis=axis, keepdims=True)
    return cen * lax.rsqrt(var + EPS)


def fused_kernel(
    rows, cols, dims,
    fam, keep, amino, amino_v, contact_any, wl, wr, w2t_any, es, et, efs, ef, fe, fs,
    out,
    rsend, lsend, prs, rbuf, lbuf, vbuf, contact, w2t,
    lf, lmat, cnts, acts, psc, lp, rp, first, gate, pns,
    lfull, rfull, prod, pbuf,
    rs_send, rs_recv, ls_send, ls_recv, lx_send, vx_send, vs_recv,
    pl_send, pl_recv, pr_send, pr_recv, pb_send, pb_recv, local,
):
    ns, tc, tr, ch, wide = dims
    x = lax.axis_index("cols")
    r = lax.axis_index("rows")
    n = rows * cols
    me = r * cols + x
    rpc = tc // tr
    outer = rows // 4
    groups = ns // PACK
    lanes = PACK * ch
    total = rows * ns
    rg = rows * groups
    own = lfull.shape[0]
    zc = es.shape[1] // 2
    mine = lax.rem(r, rpc)
    home = r // rpc
    barrier = pltpu.get_barrier_semaphore()

    def peer(t):
        other = lax.rem(me + t, n)
        return other, other // cols, lax.rem(other, cols)

    def greet(t, carry):
        _, rr, xx = peer(t)
        pl.semaphore_signal(
            barrier, inc=1, device_id={"rows": rr, "cols": xx}, device_id_type=MESH
        )
        return carry

    lax.fori_loop(1, n, greet, 0)
    load_contact = pltpu.make_async_copy(contact_any, contact, local.at[3])
    load_w2t = pltpu.make_async_copy(w2t_any, w2t, local.at[4])
    load_contact.start()
    load_w2t.start()

    cols_live = amino_v[:, pl.ds(pl.multiple_of(x * tc, tc), tc)].astype(F32)
    live = keep[...].astype(F32) * cols_live
    live_t = live.T
    for g in range(groups):
        parts = []
        for k in range(PACK):
            s = g * PACK + k
            xn = normalise(fam[s], -1).astype(BF16)
            prs[pl.ds(s, ch, stride=ns), :] = contract(wr[...], xn, 1, 1) * live[s : s + 1, :]
            parts.append(contract(xn, wl[...], 1, 1) * live_t[:, s : s + 1])
        lsend[g] = jnp.concatenate(parts, axis=1).astype(BF16)
    rsend[0:ch] = prs[...].reshape(ch, ns, tc).astype(BF16)
    rsend[ch] = live.astype(BF16)
    pl.semaphore_wait(barrier, n - 1)

    o = r // 4
    m = lax.rem(r // 2, 2)
    k = lax.rem(r, 2)

    def row_of(oo, mm, kk):
        return (oo * 2 + mm) * 2 + kk

    def rcopy(block, dst_row, sem, fresh):
        return pltpu.make_async_remote_copy(
            src_ref=rsend if fresh else rbuf.at[block],
            dst_ref=rbuf.at[block],
            send_sem=rs_send.at[sem],
            recv_sem=rs_recv.at[block],
            device_id={"rows": dst_row},
            device_id_type=MESH,
        )

    def rwait(block):
        pltpu.make_async_copy(rsend, rbuf.at[block], rs_recv.at[block]).wait()

    mate = row_of(o, m, 1 - k)
    side = row_of(o, 1 - m, k)
    sends = []
    for t in range(1, outer):
        sends.append(rcopy(r, row_of(lax.rem(o + t, outer), m, k), t - 1, True))
        sends[-1].start()
    sends.append(rcopy(r, side, outer - 1, True))
    sends[-1].start()
    sends.append(rcopy(r, mate, outer, True))
    sends[-1].start()
    own_r = pltpu.make_async_copy(rsend, rbuf.at[r], local.at[0])
    own_r.start()

    def lcopy(t):
        return pltpu.make_async_remote_copy(
            src_ref=lsend.at[:, pl.ds(pl.multiple_of(t * tr, tr), tr), :],
            dst_ref=lbuf.at[r],
            send_sem=ls_send.at[t],
            recv_sem=ls_recv.at[r],
            device_id={"rows": x * rpc + t},
            device_id_type=MESH,
        )

    def lsends(t, carry):
        @pl.when(x * rpc + t != r)
        def _():
            lcopy(t).start()

        return carry

    lax.fori_loop(0, rpc, lsends, 0)

    @pl.when(home == x)
    def _():
        a = pltpu.make_async_copy(
            lsend.at[:, pl.ds(pl.multiple_of(mine * tr, tr), tr), :], lbuf.at[r], local.at[1]
        )
        a.start()
        a.wait()

    def lwait(block):
        pltpu.make_async_copy(
            lsend.at[:, pl.ds(0, tr), :], lbuf.at[block], ls_recv.at[block]
        ).wait()

    def hand(block, step, left):
        return pltpu.make_async_remote_copy(
            src_ref=lbuf.at[block] if left else rbuf.at[block, ch],
            dst_ref=lbuf.at[block] if left else vbuf.at[block],
            send_sem=(lx_send if left else vx_send).at[block, step - 1],
            recv_sem=(ls_recv if left else vs_recv).at[block],
            device_id={"cols": lax.rem(x + step, cols)},
            device_id_type=MESH,
        )

    sem = outer + 1
    for t in range(1, outer):
        block = row_of(lax.rem(o + outer - t, outer), m, k)
        rwait(block)
        for dst in (side, mate):
            sends.append(rcopy(block, dst, sem, False))
            sends[-1].start()
            sem += 1

    @pl.when(home == x)
    def _():
        def forward(t, carry):
            block = lax.rem(r + t, rows)

            @pl.when(block != r)
            def _():
                lwait(block)

            for step in range(1, cols):
                hand(block, step, True).start()
            return carry

        lax.fori_loop(0, rows, forward, 0)

    for t in range(outer):
        block = row_of(lax.rem(o + outer - t, outer), 1 - m, k)
        rwait(block)
        sends.append(rcopy(block, mate, sem, False))
        sends[-1].start()
        sem += 1
    own_r.wait()
    for t in range(outer):
        for mm in range(2):
            rwait(row_of(lax.rem(o + outer - t, outer), mm, 1 - k))

    @pl.when(home == x)
    def _():
        def forward(block, carry):
            for step in range(1, cols):
                hand(block, step, False).start()
            return carry

        lax.fori_loop(0, rows, forward, 0)
        vbuf[...] = rbuf[:, ch]

    @pl.when(home != x)
    def _():
        def take(block, carry):
            lwait(block)
            return carry

        lax.fori_loop(0, rows, take, 0)

    lf[...] = lbuf[...].astype(F32).reshape(rg * tr, lanes)
    place = (
        lax.broadcasted_iota(jnp.int32, (rg, total), 1) // PACK
        == lax.broadcasted_iota(jnp.int32, (rg, total), 0)
    ).astype(F32).astype(BF16)
    pick = lax.rem(
        lax.broadcasted_iota(jnp.int32, (lanes, total), 1), PACK
    ) == lax.broadcasted_iota(jnp.int32, (lanes, total), 0) // ch
    for i in range(tr):
        y = contract(lf[pl.ds(i, rg, stride=tr), :].astype(BF16), place, 0, 0)
        y = jnp.where(pick, y, 0.0)
        acc = y[0:ch]
        for q in range(1, PACK):
            acc = acc + y[q * ch : (q + 1) * ch]
        lmat[i * ch : (i + 1) * ch, :] = acc.astype(BF16)

    @pl.when(home != x)
    def _():
        def take(block, carry):
            pltpu.make_async_copy(rsend.at[ch], vbuf.at[block], vs_recv.at[block]).wait()
            return carry

        lax.fori_loop(0, rows, take, 0)

    v_left = vbuf[...].astype(F32).reshape(total, tc).astype(BF16)
    v_right = rbuf[:, ch].astype(F32).reshape(total, tc).astype(BF16)
    cnts[...] = contract(v_left, v_right, 0, 0)
    inv = 1.0 / jnp.maximum(cnts[pl.ds(pl.multiple_of(mine * tr, tr), tr), :], 1.0)

    def outer_step(d, carry):
        rd = rbuf[:, d].astype(F32).reshape(total, tc).astype(BF16)
        a = jnp.dot(lmat[...], rd, preferred_element_type=F32).reshape(tr, ch, tc)
        acts[:, pl.ds(pl.multiple_of(d * ch, ch), ch), :] = (a * inv[:, None, :]).astype(BF16)
        return carry

    lax.fori_loop(0, ch, outer_step, 0, unroll=4)
    load_contact.wait()
    load_w2t.wait()

    def mask_of(g):
        return jnp.concatenate(
            [cols_live * amino[r * tr + g * wide + i].astype(F32) for i in range(wide)], axis=1
        )

    def panel_of(weight, pn, g):
        raw = contract(weight[...], pn, 0, 0)
        val = raw[:zc] * jax.nn.sigmoid(raw[zc:]) * mask_of(g)
        for i in range(wide):
            psc[pl.ds(g * wide + i, zc, stride=tr), :] = val[:, i * tc : (i + 1) * tc]

    for g in range(tr // wide):
        base = g * wide
        u = jnp.dot(
            w2t[...],
            jnp.concatenate([acts[base + i] for i in range(wide)], axis=1),
            preferred_element_type=F32,
        )
        f = jnp.concatenate([contact[base + i].T for i in range(wide)], axis=1) + u
        first[g] = f
        pn = normalise(f, 0).astype(BF16)
        pns[g] = pn
        panel_of(es, pn, g)
    lp[...] = psc[...].reshape(zc, tr, tc).astype(BF16)

    def tile(ref, rr, xx):
        return ref.at[
            pl.ds(pl.multiple_of(rr * tr, tr), tr), pl.ds(pl.multiple_of(xx * tc, tc), tc)
        ]

    def left_copy(t):
        other, rr, xx = peer(t)
        return pltpu.make_async_remote_copy(
            src_ref=lp.at[pl.ds(other * own, own)],
            dst_ref=lfull.at[
                :, pl.ds(pl.multiple_of(r * tr, tr), tr), pl.ds(pl.multiple_of(x * tc, tc), tc)
            ],
            send_sem=pl_send.at[t],
            recv_sem=pl_recv.at[t],
            device_id={"rows": rr, "cols": xx},
            device_id_type=MESH,
        )

    def right_copy(c, t):
        other, rr, xx = peer(t)
        return pltpu.make_async_remote_copy(
            src_ref=rp.at[other * own + c],
            dst_ref=tile(rfull.at[c], r, x),
            send_sem=pr_send.at[c, t],
            recv_sem=pr_recv.at[c, t],
            device_id={"rows": rr, "cols": xx},
            device_id_type=MESH,
        )

    def back_copy(c, t):
        _, rr, xx = peer(t)
        return pltpu.make_async_remote_copy(
            src_ref=tile(prod.at[c], rr, xx),
            dst_ref=pbuf.at[me * own + c],
            send_sem=pb_send.at[c, t],
            recv_sem=pb_recv.at[c, t],
            device_id={"rows": rr, "cols": xx},
            device_id_type=MESH,
        )

    def each(fn):
        def step(t, carry):
            fn(t)
            return carry

        lax.fori_loop(1, n, step, 0)

    each(lambda t: left_copy(t).start())
    own_l = pltpu.make_async_copy(
        lp.at[pl.ds(me * own, own)],
        lfull.at[:, pl.ds(pl.multiple_of(r * tr, tr), tr), pl.ds(pl.multiple_of(x * tc, tc), tc)],
        local.at[0],
    )
    own_l.start()
    for g in range(tr // wide):
        panel_of(et, pns[g], g)
    rp[...] = psc[...].reshape(zc, tr, tc).astype(BF16)
    for c in range(min(2, own)):
        each(lambda t: right_copy(c, t).start())
    own_p = []
    for c in range(own):
        own_p.append(
            pltpu.make_async_copy(rp.at[me * own + c], tile(rfull.at[c], r, x), local.at[5 + c])
        )
        own_p[-1].start()
    for g in range(tr // wide):
        gate[g] = jax.nn.sigmoid(contract(efs[...], pns[g], 0, 0))
    own_l.wait()

    def left_wait(t):
        _, rr, xx = peer(n - t)
        pltpu.make_async_copy(
            lp.at[pl.ds(0, own)],
            lfull.at[
                :, pl.ds(pl.multiple_of(rr * tr, tr), tr), pl.ds(pl.multiple_of(xx * tc, tc), tc)
            ],
            pl_recv.at[t],
        ).wait()

    def right_wait(c, t):
        _, rr, xx = peer(n - t)
        pltpu.make_async_copy(rp.at[0], tile(rfull.at[c], rr, xx), pr_recv.at[c, t]).wait()

    def back_wait(c, t):
        src, _, _ = peer(n - t)
        pltpu.make_async_copy(rp.at[0], pbuf.at[src * own + c], pb_recv.at[c, t]).wait()

    each(left_wait)
    own_b = []
    for c in range(own):
        own_p[c].wait()
        each(lambda t: right_wait(c, t))
        prod[c] = contract(lfull[c], rfull[c], 1, 1).astype(BF16)
        if c + 2 < own:
            each(lambda t: right_copy(c + 2, t).start())
        each(lambda t: back_copy(c, t).start())
        own_b.append(
            pltpu.make_async_copy(
                tile(prod.at[c], r, x), pbuf.at[me * own + c], local.at[5 + own + c]
            )
        )
        own_b[-1].start()

    for s in sends:
        s.wait_send()

    def lsent(t, carry):
        @pl.when(x * rpc + t != r)
        def _():
            lcopy(t).wait_send()

        return carry

    lax.fori_loop(0, rpc, lsent, 0)

    @pl.when(home == x)
    def _():
        def sent(block, carry):
            for step in range(1, cols):
                hand(block, step, True).wait_send()
                hand(block, step, False).wait_send()
            return carry

        lax.fori_loop(0, rows, sent, 0)

    each(lambda t: left_copy(t).wait_send())
    for c in range(own):
        each(lambda t: right_copy(c, t).wait_send())
    for c in range(own):
        own_b[c].wait()
        each(lambda t: back_wait(c, t))

    psc[...] = normalise(pbuf[...].astype(F32), 0).reshape(zc * tr, tc)
    for g in range(tr // wide):
        mixed = jnp.concatenate(
            [psc[pl.ds(g * wide + i, zc, stride=tr), :].astype(BF16) for i in range(wide)], axis=1
        )
        second = first[g] + gate[g] * contract(ef[...], mixed, 0, 0)
        tn = normalise(second, 0).astype(BF16)
        hidden = jax.nn.relu(contract(fe[...], tn, 0, 0)).astype(BF16)
        res = second + contract(fs[...], hidden, 0, 0)
        for i in range(wide):
            out[g * wide + i] = res[:, i * tc : (i + 1) * tc].T
    for c in range(own):
        each(lambda t: back_copy(c, t).wait_send())


def on_device(fam, keep, amino, contact, wl, wr, pf, es, et, efs, ef, fe, fs):
    rows = lax.axis_size("rows")
    cols = lax.axis_size("cols")
    ns, tc, _ = fam.shape
    tr, _, z = contact.shape
    ch = wl.shape[1]
    zc = es.shape[1] // 2
    groups = ns // PACK
    lanes = PACK * ch
    n = rows * cols
    own = zc // n
    rpc = tc // tr
    total = rows * ns
    wide = 4
    outer = rows // 4
    dma = pltpu.SemaphoreType.DMA
    vmem = pltpu.VMEM
    w2t = pf.reshape(ch, ch, z).transpose(2, 1, 0).reshape(z, ch * ch)
    nsem = outer + 1 + 2 * (outer - 1) + outer
    full = (own, rows * tr, cols * tc)
    return pl.pallas_call(
        functools.partial(fused_kernel, rows, cols, (ns, tc, tr, ch, wide)),
        out_shape=jax.ShapeDtypeStruct((tr, tc, z), F32),
        in_specs=[VM, VM, SM, VM, ANY, VM, VM, ANY] + [VM] * 6,
        out_specs=VM,
        scratch_shapes=[
            vmem((ch + 1, ns, tc), BF16),
            vmem((groups, tc, lanes), BF16),
            vmem((ch * ns, tc), F32),
            vmem((rows, ch + 1, ns, tc), BF16),
            vmem((rows, groups, tr, lanes), BF16),
            vmem((rows, ns, tc), BF16),
            vmem((tr, tc, z), F32),
            vmem((z, ch * ch), BF16),
            vmem((rows * groups * tr, lanes), F32),
            vmem((tr * ch, total), BF16),
            vmem((tc, tc), F32),
            vmem((tr, ch * ch, tc), BF16),
            vmem((zc * tr, tc), F32),
            vmem((zc, tr, tc), BF16),
            vmem((zc, tr, tc), BF16),
            vmem((tr // wide, z, wide * tc), F32),
            vmem((tr // wide, z, wide * tc), F32),
            vmem((tr // wide, z, wide * tc), BF16),
            vmem(full, BF16),
            vmem(full, BF16),
            vmem(full, BF16),
            vmem((zc, tr, tc), BF16),
            dma((nsem,)),
            dma((rows,)),
            dma((rpc,)),
            dma((rows,)),
            dma((rows, cols - 1)),
            dma((rows, cols - 1)),
            dma((rows,)),
            dma((n,)),
            dma((n,)),
            dma((own, n)),
            dma((own, n)),
            dma((own, n)),
            dma((own, n)),
            dma((5 + 2 * own,)),
        ],
        compiler_params=pltpu.CompilerParams(
            vmem_limit_bytes=60 * 1024 * 1024, collective_id=0, has_side_effects=True
        ),
        name="pair_block",
    )(fam, keep, amino, amino.reshape(1, -1), contact, wl.T, wr.T, w2t, es, et, efs, ef, fe, fs)


def solution(mesh):
    tile3 = P(("crops", "rows"), "cols", None)
    in_specs = (tile3, P(("crops", "rows"), "cols"), P("crops"), tile3) + (P(),) * 9
    return jax.shard_map(
        on_device, mesh=mesh, in_specs=in_specs, out_specs=tile3, check_vma=False
    )
```

time: 100 us -> 81.4 us (0.81)
  the two profiles are of different devices: /device:TPU:21 before, /device:TPU:0 now
where the time goes in v2:
time: 81.4 us; the launch traced here: 81.2 us
  Pallas kernels  77 us (95%)
  local copies, waits for them, and re-layouts  4.2 us (5%)
    pallas_call x1, Pallas kernels, on_device(): pl.pallas_call(functools.partial(fused_kernel, rows, cols, (ns, tc, tr, c...  77 us
    unnamed x1, local copies, waits for them, and re-layouts  2.3 us

profile of v2, /device:TPU:0, one launch (start us, length us, event | category | flops | bytes accessed | tf_op | source)
XLA Modules:
  0.0 81.2 jit_solution(7563308028073058443)
XLA Ops:
  0.0 1.1 %copy.16 = bf16[128,32,32]{0,2,1:T(8,128)(2,1)S(1)} copy(bf16[128,32,32]{0,1,2:T(8,128)(2,1)} %bitcast.8) | data formatting | bytes 524288 | tf_op jit(solution)/shard_map/transpose | solution.py:446
  1.1 0.9 %copy.17.w2t_any = bf16[128,1024]{1,0:T(8,128)(2,1)} copy(bf16[128,1024]{0,1:T(8,128)(2,1)S(1)} %bitcast.7) | data formatting | bytes 524288 | tf_op jit(solution)/shard_map/reshape | solution.py:446
  1.9 77.0 %pair_block.1 = f32[16,128,128]{2,1,0:T(8,128)} custom-call(f32[8,128,256]{2,1,0:T(8,128)} %fam.1, s32[8,128]{1,0:T(8,128)} %keep.1, s32[256]{0:T(256)} %amino.1, s32[1,256]{1,0:T(1,128)} %bitcast.11, f32[16,128,128]{2,1,0:T(8,128)} %contact_any.1, bf16[32,256]{1,0:T(8,128)(2,1)} %bitcast.9, bf16[32,256]{1,0:T(8,128)(2,1)} %bitcast.10, ...), custom_call_target="tpu_custom_call" | custom-call | tf_op jit(solution)/shard_map/pair_block/pallas_call | solution.py:449
  78.9 2.3 %copy.19 = f32[16,128,128]{2,1,0:T(8,128)} copy(f32[16,128,128]{2,1,0:T(8,128)} %pair_block.1) | data formatting | bytes 2097152

commit v3 on v2

--- a/solution.py
+++ b/solution.py
@@ -30,9 +30,9 @@
 
 def fused_kernel(
     rows, cols, dims,
-    fam, keep, amino, amino_v, contact_any, wl, wr, w2t_any, es, et, efs, ef, fe, fs,
+    fam, keep, amino, amino_v, contact_any, wl, wr, pf_any, es, et, efs, ef, fe, fs,
     out,
-    rsend, lsend, prs, rbuf, lbuf, vbuf, contact, w2t,
+    rsend, lsend, prs, rbuf, lbuf, vbuf, contact, pf, pf_wide, w2t,
     lf, lmat, cnts, acts, psc, lp, rp, first, gate, pns,
     lfull, rfull, prod, pbuf,
     rs_send, rs_recv, ls_send, ls_recv, lx_send, vx_send, vs_recv,
@@ -68,9 +68,9 @@
 
     lax.fori_loop(1, n, greet, 0)
     load_contact = pltpu.make_async_copy(contact_any, contact, local.at[3])
-    load_w2t = pltpu.make_async_copy(w2t_any, w2t, local.at[4])
+    load_pf = pltpu.make_async_copy(pf_any, pf, local.at[4])
     load_contact.start()
-    load_w2t.start()
+    load_pf.start()
 
     cols_live = amino_v[:, pl.ds(pl.multiple_of(x * tc, tc), tc)].astype(F32)
     live = keep[...].astype(F32) * cols_live
@@ -147,17 +147,39 @@
         a.start()
         a.wait()
 
+    def vcopy(t, step):
+        return pltpu.make_async_remote_copy(
+            src_ref=rsend.at[ch],
+            dst_ref=vbuf.at[r],
+            send_sem=vx_send.at[t, step - 1],
+            recv_sem=vs_recv.at[r],
+            device_id={"rows": x * rpc + t, "cols": lax.rem(x + step, cols)},
+            device_id_type=MESH,
+        )
+
+    def vsends(t, carry):
+        for step in range(1, cols):
+            vcopy(t, step).start()
+        return carry
+
+    lax.fori_loop(0, rpc, vsends, 0)
+
+    load_pf.wait()
+    pf_wide[...] = pf[...].astype(F32)
+    for d in range(ch):
+        w2t[d * ch : (d + 1) * ch, :] = pf_wide[pl.ds(d, ch, stride=ch), :].astype(BF16)
+
     def lwait(block):
         pltpu.make_async_copy(
             lsend.at[:, pl.ds(0, tr), :], lbuf.at[block], ls_recv.at[block]
         ).wait()
 
-    def hand(block, step, left):
-        return pltpu.make_async_remote_copy(
-            src_ref=lbuf.at[block] if left else rbuf.at[block, ch],
-            dst_ref=lbuf.at[block] if left else vbuf.at[block],
-            send_sem=(lx_send if left else vx_send).at[block, step - 1],
-            recv_sem=(ls_recv if left else vs_recv).at[block],
+    def hand(block, step):
+        return pltpu.make_async_remote_copy(
+            src_ref=lbuf.at[block],
+            dst_ref=lbuf.at[block],
+            send_sem=lx_send.at[block, step - 1],
+            recv_sem=ls_recv.at[block],
             device_id={"cols": lax.rem(x + step, cols)},
             device_id_type=MESH,
         )
@@ -181,7 +203,7 @@
                 lwait(block)
 
             for step in range(1, cols):
-                hand(block, step, True).start()
+                hand(block, step).start()
             return carry
 
         lax.fori_loop(0, rows, forward, 0)
@@ -192,21 +214,6 @@
         sends.append(rcopy(block, mate, sem, False))
         sends[-1].start()
         sem += 1
-    own_r.wait()
-    for t in range(outer):
-        for mm in range(2):
-            rwait(row_of(lax.rem(o + outer - t, outer), mm, 1 - k))
-
-    @pl.when(home == x)
-    def _():
-        def forward(block, carry):
-            for step in range(1, cols):
-                hand(block, step, False).start()
-            return carry
-
-        lax.fori_loop(0, rows, forward, 0)
-        vbuf[...] = rbuf[:, ch]
-
     @pl.when(home != x)
     def _():
         def take(block, carry):
@@ -239,20 +246,34 @@
 
         lax.fori_loop(0, rows, take, 0)
 
+    own_r.wait()
+    for t in range(outer):
+        for mm in range(2):
+            rwait(row_of(lax.rem(o + outer - t, outer), mm, 1 - k))
+
+    @pl.when(home == x)
+    def _():
+        vbuf[...] = rbuf[:, ch]
+
     v_left = vbuf[...].astype(F32).reshape(total, tc).astype(BF16)
     v_right = rbuf[:, ch].astype(F32).reshape(total, tc).astype(BF16)
     cnts[...] = contract(v_left, v_right, 0, 0)
     inv = 1.0 / jnp.maximum(cnts[pl.ds(pl.multiple_of(mine * tr, tr), tr), :], 1.0)
 
-    def outer_step(d, carry):
-        rd = rbuf[:, d].astype(F32).reshape(total, tc).astype(BF16)
-        a = jnp.dot(lmat[...], rd, preferred_element_type=F32).reshape(tr, ch, tc)
-        acts[:, pl.ds(pl.multiple_of(d * ch, ch), ch), :] = (a * inv[:, None, :]).astype(BF16)
+    def slab(d):
+        return rbuf[:, d].astype(F32).reshape(total, tc).astype(BF16)
+
+    def outer_step(h, carry):
+        rd = jnp.concatenate([slab(2 * h), slab(2 * h + 1)], axis=1)
+        a = jnp.dot(lmat[...], rd, preferred_element_type=F32)
+        for q in range(2):
+            part = a[:, q * tc : (q + 1) * tc].reshape(tr, ch, tc) * inv[:, None, :]
+            at = pl.multiple_of((2 * h + q) * ch, ch)
+            acts[:, pl.ds(at, ch), :] = part.astype(BF16)
         return carry
 
-    lax.fori_loop(0, ch, outer_step, 0, unroll=4)
+    lax.fori_loop(0, ch // 2, outer_step, 0, unroll=2)
     load_contact.wait()
-    load_w2t.wait()
 
     def mask_of(g):
         return jnp.concatenate(
@@ -267,10 +288,8 @@
 
     for g in range(tr // wide):
         base = g * wide
-        u = jnp.dot(
-            w2t[...],
-            jnp.concatenate([acts[base + i] for i in range(wide)], axis=1),
-            preferred_element_type=F32,
+        u = contract(
+            w2t[...], jnp.concatenate([acts[base + i] for i in range(wide)], axis=1), 0, 0
         )
         f = jnp.concatenate([contact[base + i].T for i in range(wide)], axis=1) + u
         first[g] = f
@@ -390,6 +409,8 @@
         def _():
             lcopy(t).wait_send()
 
+        for step in range(1, cols):
+            vcopy(t, step).wait_send()
         return carry
 
     lax.fori_loop(0, rpc, lsent, 0)
@@ -398,8 +419,7 @@
     def _():
         def sent(block, carry):
             for step in range(1, cols):
-                hand(block, step, True).wait_send()
-                hand(block, step, False).wait_send()
+                hand(block, step).wait_send()
             return carry
 
         lax.fori_loop(0, rows, sent, 0)
@@ -443,7 +463,6 @@
     outer = rows // 4
     dma = pltpu.SemaphoreType.DMA
     vmem = pltpu.VMEM
-    w2t = pf.reshape(ch, ch, z).transpose(2, 1, 0).reshape(z, ch * ch)
     nsem = outer + 1 + 2 * (outer - 1) + outer
     full = (own, rows * tr, cols * tc)
     return pl.pallas_call(
@@ -459,7 +478,9 @@
             vmem((rows, groups, tr, lanes), BF16),
             vmem((rows, ns, tc), BF16),
             vmem((tr, tc, z), F32),
-            vmem((z, ch * ch), BF16),
+            vmem((ch * ch, z), BF16),
+            vmem((ch * ch, z), F32),
+            vmem((ch * ch, z), BF16),
             vmem((rows * groups * tr, lanes), F32),
             vmem((tr * ch, total), BF16),
             vmem((tc, tc), F32),
@@ -479,7 +500,7 @@
             dma((rpc,)),
             dma((rows,)),
             dma((rows, cols - 1)),
-            dma((rows, cols - 1)),
+            dma((rpc, cols - 1)),
             dma((rows,)),
             dma((n,)),
             dma((n,)),
@@ -493,7 +514,7 @@
             vmem_limit_bytes=60 * 1024 * 1024, collective_id=0, has_side_effects=True
         ),
         name="pair_block",
-    )(fam, keep, amino, amino.reshape(1, -1), contact, wl.T, wr.T, w2t, es, et, efs, ef, fe, fs)
+    )(fam, keep, amino, amino.reshape(1, -1), contact, wl.T, wr.T, pf, es, et, efs, ef, fe, fs)
 
 
 def solution(mesh):

time: 81.4 us -> 79.9 us (0.982)
  local copies, waits for them, and re-layouts: 4.2 us -> 2.3 us
    transpose x1 -> x0, local copies, waits for them, and re-layouts: 1.05 us -> none  [on_device(): w2t = pf.reshape(ch, ch, z).transpose(2, 1, 0).reshape(z, ch * ch)]
    reshape x1 -> x0, local copies, waits for them, and re-layouts: 0.85 us -> none  [on_device(): w2t = pf.reshape(ch, ch, z).transpose(2, 1, 0).reshape(z, ch * ch)]
where the time goes in v3:
time: 79.9 us; the launch traced here: 79.7 us
  Pallas kernels  77.4 us (97%)
  local copies, waits for them, and re-layouts  2.3 us (3%)
    pallas_call x1, Pallas kernels, on_device(): pl.pallas_call(functools.partial(fused_kernel, rows, cols, (ns, tc, tr, c...  77.4 us
    unnamed x1, local copies, waits for them, and re-layouts  2.3 us

profile of v3, /device:TPU:0, one launch (start us, length us, event | category | flops | bytes accessed | tf_op | source)
XLA Modules:
  0.0 79.7 jit_solution(5428500333039923444)
XLA Ops:
  0.0 77.4 %pair_block.1 = f32[16,128,128]{2,1,0:T(8,128)} custom-call(f32[8,128,256]{2,1,0:T(8,128)} %fam.1, s32[8,128]{1,0:T(8,128)} %keep.1, s32[256]{0:T(256)} %amino.1, s32[1,256]{1,0:T(1,128)} %bitcast.5, f32[16,128,128]{2,1,0:T(8,128)} %contact_any.1, bf16[32,256]{1,0:T(8,128)(2,1)} %bitcast.3, bf16[32,256]{1,0:T(8,128)(2,1)} %bitcast.4, ...), custom_call_target="tpu_custom_call" | custom-call | tf_op jit(solution)/shard_map/pair_block/pallas_call | solution.py:468
  77.4 2.3 %copy.15 = f32[16,128,128]{2,1,0:T(8,128)} copy(f32[16,128,128]{2,1,0:T(8,128)} %pair_block.1) | data formatting | bytes 2097152

commit v4 on v3

--- a/solution.py
+++ b/solution.py
@@ -1,4 +1,5 @@
 import functools
+import math
 
 import jax
 import jax.numpy as jnp
@@ -32,7 +33,7 @@
     rows, cols, dims,
     fam, keep, amino, amino_v, contact_any, wl, wr, pf_any, es, et, efs, ef, fe, fs,
     out,
-    rsend, lsend, prs, rbuf, lbuf, vbuf, contact, pf, pf_wide, w2t,
+    rsend, lsend, prs, rbuf, lbuf, vbuf, contact, pf, pf_wide, pf_dc, w2t,
     lf, lmat, cnts, acts, psc, lp, rp, first, gate, pns,
     lfull, rfull, prod, pbuf,
     rs_send, rs_recv, ls_send, ls_recv, lx_send, vx_send, vs_recv,
@@ -53,10 +54,13 @@
     zc = es.shape[1] // 2
     mine = lax.rem(r, rpc)
     home = r // rpc
+    stride = n // 4 + 1
+    while math.gcd(stride, n) != 1:
+        stride += 1
     barrier = pltpu.get_barrier_semaphore()
 
     def peer(t):
-        other = lax.rem(me + t, n)
+        other = lax.rem(me + t * stride, n)
         return other, other // cols, lax.rem(other, cols)
 
     def greet(t, carry):
@@ -167,7 +171,7 @@
     load_pf.wait()
     pf_wide[...] = pf[...].astype(F32)
     for d in range(ch):
-        w2t[d * ch : (d + 1) * ch, :] = pf_wide[pl.ds(d, ch, stride=ch), :].astype(BF16)
+        pf_dc[d * ch : (d + 1) * ch, :] = pf_wide[pl.ds(d, ch, stride=ch), :]
 
     def lwait(block):
         pltpu.make_async_copy(
@@ -246,6 +250,8 @@
 
         lax.fori_loop(0, rows, take, 0)
 
+    for q in range(0, ch * ch, tc):
+        w2t[:, q : q + tc] = pf_dc[q : q + tc, :].T.astype(BF16)
     own_r.wait()
     for t in range(outer):
         for mm in range(2):
@@ -288,8 +294,10 @@
 
     for g in range(tr // wide):
         base = g * wide
-        u = contract(
-            w2t[...], jnp.concatenate([acts[base + i] for i in range(wide)], axis=1), 0, 0
+        u = jnp.dot(
+            w2t[...],
+            jnp.concatenate([acts[base + i] for i in range(wide)], axis=1),
+            preferred_element_type=F32,
         )
         f = jnp.concatenate([contact[base + i].T for i in range(wide)], axis=1) + u
         first[g] = f
@@ -480,7 +488,8 @@
             vmem((tr, tc, z), F32),
             vmem((ch * ch, z), BF16),
             vmem((ch * ch, z), F32),
-            vmem((ch * ch, z), BF16),
+            vmem((ch * ch, z), F32),
+            vmem((z, ch * ch), BF16),
             vmem((rows * groups * tr, lanes), F32),
             vmem((tr * ch, total), BF16),
             vmem((tc, tc), F32),

time: 79.9 us -> 79.6 us (level)
  no operation moved by 1% of the time
where the time goes in v4:
time: 79.6 us; the launch traced here: 79.4 us
  Pallas kernels  77.1 us (97%)
  local copies, waits for them, and re-layouts  2.3 us (3%)
    pallas_call x1, Pallas kernels, on_device(): pl.pallas_call(functools.partial(fused_kernel, rows, cols, (ns, tc, tr, c...  77.1 us
    unnamed x1, local copies, waits for them, and re-layouts  2.3 us

profile of v4, /device:TPU:0, one launch (start us, length us, event | category | flops | bytes accessed | tf_op | source)
XLA Modules:
  0.0 79.4 jit_solution(13908074008565655825)
XLA Ops:
  0.0 77.1 %pair_block.1 = f32[16,128,128]{2,1,0:T(8,128)} custom-call(f32[8,128,256]{2,1,0:T(8,128)} %fam.1, s32[8,128]{1,0:T(8,128)} %keep.1, s32[256]{0:T(256)} %amino.1, s32[1,256]{1,0:T(1,128)} %bitcast.5, f32[16,128,128]{2,1,0:T(8,128)} %contact_any.1, bf16[32,256]{1,0:T(8,128)(2,1)} %bitcast.3, bf16[32,256]{1,0:T(8,128)(2,1)} %bitcast.4, ...), custom_call_target="tpu_custom_call" | custom-call | tf_op jit(solution)/shard_map/pair_block/pallas_call | solution.py:476
  77.1 2.3 %copy.15 = f32[16,128,128]{2,1,0:T(8,128)} copy(f32[16,128,128]{2,1,0:T(8,128)} %pair_block.1) | data formatting | bytes 2097152

commit v5 on v4

--- a/solution.py
+++ b/solution.py
@@ -318,8 +318,8 @@
             dst_ref=lfull.at[
                 :, pl.ds(pl.multiple_of(r * tr, tr), tr), pl.ds(pl.multiple_of(x * tc, tc), tc)
             ],
-            send_sem=pl_send.at[t],
-            recv_sem=pl_recv.at[t],
+            send_sem=pl_send.at[0],
+            recv_sem=pl_recv.at[0],
             device_id={"rows": rr, "cols": xx},
             device_id_type=MESH,
         )
@@ -329,8 +329,8 @@
         return pltpu.make_async_remote_copy(
             src_ref=rp.at[other * own + c],
             dst_ref=tile(rfull.at[c], r, x),
-            send_sem=pr_send.at[c, t],
-            recv_sem=pr_recv.at[c, t],
+            send_sem=pr_send.at[c],
+            recv_sem=pr_recv.at[c],
             device_id={"rows": rr, "cols": xx},
             device_id_type=MESH,
         )
@@ -340,8 +340,8 @@
         return pltpu.make_async_remote_copy(
             src_ref=tile(prod.at[c], rr, xx),
             dst_ref=pbuf.at[me * own + c],
-            send_sem=pb_send.at[c, t],
-            recv_sem=pb_recv.at[c, t],
+            send_sem=pb_send.at[c],
+            recv_sem=pb_recv.at[c],
             device_id={"rows": rr, "cols": xx},
             device_id_type=MESH,
         )
@@ -375,29 +375,14 @@
         gate[g] = jax.nn.sigmoid(contract(efs[...], pns[g], 0, 0))
     own_l.wait()
 
-    def left_wait(t):
-        _, rr, xx = peer(n - t)
-        pltpu.make_async_copy(
-            lp.at[pl.ds(0, own)],
-            lfull.at[
-                :, pl.ds(pl.multiple_of(rr * tr, tr), tr), pl.ds(pl.multiple_of(xx * tc, tc), tc)
-            ],
-            pl_recv.at[t],
-        ).wait()
-
-    def right_wait(c, t):
-        _, rr, xx = peer(n - t)
-        pltpu.make_async_copy(rp.at[0], tile(rfull.at[c], rr, xx), pr_recv.at[c, t]).wait()
-
-    def back_wait(c, t):
-        src, _, _ = peer(n - t)
-        pltpu.make_async_copy(rp.at[0], pbuf.at[src * own + c], pb_recv.at[c, t]).wait()
-
-    each(left_wait)
+    def take_all(sem, tiles):
+        pltpu.make_async_copy(lp.at[pl.ds(0, tiles)], pbuf.at[pl.ds(0, tiles)], sem).wait()
+
+    take_all(pl_recv.at[0], (n - 1) * own)
     own_b = []
     for c in range(own):
         own_p[c].wait()
-        each(lambda t: right_wait(c, t))
+        take_all(pr_recv.at[c], n - 1)
         prod[c] = contract(lfull[c], rfull[c], 1, 1).astype(BF16)
         if c + 2 < own:
             each(lambda t: right_copy(c + 2, t).start())
@@ -432,12 +417,12 @@
 
         lax.fori_loop(0, rows, sent, 0)
 
-    each(lambda t: left_copy(t).wait_send())
+    take_all(pl_send.at[0], (n - 1) * own)
     for c in range(own):
-        each(lambda t: right_copy(c, t).wait_send())
+        take_all(pr_send.at[c], n - 1)
     for c in range(own):
         own_b[c].wait()
-        each(lambda t: back_wait(c, t))
+        take_all(pb_recv.at[c], n - 1)
 
     psc[...] = normalise(pbuf[...].astype(F32), 0).reshape(zc * tr, tc)
     for g in range(tr // wide):
@@ -451,7 +436,7 @@
         for i in range(wide):
             out[g * wide + i] = res[:, i * tc : (i + 1) * tc].T
     for c in range(own):
-        each(lambda t: back_copy(c, t).wait_send())
+        take_all(pb_send.at[c], n - 1)
 
 
 def on_device(fam, keep, amino, contact, wl, wr, pf, es, et, efs, ef, fe, fs):
@@ -511,12 +496,12 @@
             dma((rows, cols - 1)),
             dma((rpc, cols - 1)),
             dma((rows,)),
-            dma((n,)),
-            dma((n,)),
-            dma((own, n)),
-            dma((own, n)),
-            dma((own, n)),
-            dma((own, n)),
+            dma((1,)),
+            dma((1,)),
+            dma((own,)),
+            dma((own,)),
+            dma((own,)),
+            dma((own,)),
             dma((5 + 2 * own,)),
         ],
         compiler_params=pltpu.CompilerParams(

time: 79.6 us -> 73.8 us (0.927)
  Pallas kernels: 77.1 us -> 71.3 us
    pallas_call x1, Pallas kernels: 77.1 us -> 71.3 us  [on_device(): pl.pallas_call(functools.partial(fused_kernel, rows, cols, (ns, tc, tr, c...]
where the time goes in v5:
time: 73.8 us; the launch traced here: 73.6 us
  Pallas kernels  71.3 us (97%)
  local copies, waits for them, and re-layouts  2.3 us (3%)
    pallas_call x1, Pallas kernels, on_device(): pl.pallas_call(functools.partial(fused_kernel, rows, cols, (ns, tc, tr, c...  71.3 us
    unnamed x1, local copies, waits for them, and re-layouts  2.3 us

profile of v5, /device:TPU:0, one launch (start us, length us, event | category | flops | bytes accessed | tf_op | source)
XLA Modules:
  0.0 73.6 jit_solution(4190304542267104801)
XLA Ops:
  0.0 71.3 %pair_block.1 = f32[16,128,128]{2,1,0:T(8,128)} custom-call(f32[8,128,256]{2,1,0:T(8,128)} %fam.1, s32[8,128]{1,0:T(8,128)} %keep.1, s32[256]{0:T(256)} %amino.1, s32[1,256]{1,0:T(1,128)} %bitcast.5, f32[16,128,128]{2,1,0:T(8,128)} %contact_any.1, bf16[32,256]{1,0:T(8,128)(2,1)} %bitcast.3, bf16[32,256]{1,0:T(8,128)(2,1)} %bitcast.4, ...), custom_call_target="tpu_custom_call" | custom-call | tf_op jit(solution)/shard_map/pair_block/pallas_call | solution.py:461
  71.3 2.3 %copy.15 = f32[16,128,128]{2,1,0:T(8,128)} copy(f32[16,128,128]{2,1,0:T(8,128)} %pair_block.1) | data formatting | bytes 2097152
